TPU v7x, 512 devices: a whole 4x8x8 slice. The times are simulated.
512 devices in a mesh: shard: 128 (over y, z_hi, x), tensor: 4 (over z_lo, core).
Axes of the slice: x: 4, y: 8, z: 8 (z_hi: 4, z_lo: 2; z = z_hi * 2 + z_lo), core: 2. Of those that a mesh axis runs over, the one named last changes fastest.
Arguments:
- gradients: bfloat16 [128, 128, 32, 512], P('shard', None, 'tensor'), may hold values from -2 to 2
- master_weights: float32 [128, 32, 512], P('shard', 'tensor'), may hold values from -6 to 6
- first_moment: float32 [128, 32, 512], P('shard', 'tensor'), may hold values from -4 to 4
- second_moment: float32 [128, 32, 512], P('shard', 'tensor'), may hold values from 0.5 to 4
- old_basis: float32 [128, 512, 512], P('shard', 'tensor')
- old_stats: float32 [128, 512, 512], P('shard', 'tensor'), as said below
- owner_table: int32 [128], replicated, may hold values from 0 to 127, each once
Outputs:
- updated_weights: float32 [128, 32, 512], P(None, 'tensor')
- new_first: float32 [128, 32, 512], P('shard', 'tensor')
- new_second: float32 [128, 32, 512], P('shard', 'tensor')
- new_basis: float32 [128, 512, 512], P('shard', 'tensor')
- new_stats: float32 [128, 512, 512], P('shard', 'tensor')
Inputs may be any that keep to these rules, and one draw needn't show every extreme that they name: owner_table names every owner 0 to 127 exactly once. `old_stats`: each block's matrix is symmetric.
All inputs are finite; a program needn't handle non-finite values.
Results may differ from a plain program's by a relative error of at most 0.004.
Values may be sent and summed in bfloat16 or wider, within the bound.
No kernel may reach another device: no remote copies, remote signals or barrier semaphores. Data moves between devices by JAX's collectives and lax.ppermute only.
A program may use at most 64 MiB of HBM per device.

v0:
```python
import jax
import jax.numpy as jnp
from jax import lax
from jax.sharding import PartitionSpec as P

NS_ITERS = 3
momentum_decay = 0.9
square_decay = 0.95
stats_decay = 0.95
step_size = 0.05
start_gain = 1.7
epsilon = 1e-06


def gram_of(matrix):
    return lax.dot_general(
        matrix, matrix, (((0,), (0,)), ((), ())), precision=lax.Precision.HIGHEST
    )


def body(gradients, master_weights, first_moment, second_moment, old_basis, old_stats, owner_table):
    highest = lax.Precision.HIGHEST
    blocks = owner_table.shape[0]
    places = jnp.arange(blocks, dtype=jnp.int32)
    inverse = jnp.sum(
        jnp.where(owner_table[None, :] == places[:, None], places[None, :], 0), axis=1
    )
    ordered = jnp.take(gradients[0], inverse, axis=0)
    summed = lax.psum_scatter(
        ordered.astype(jnp.float32), "shard", scatter_dimension=0, tiled=True
    )[0]
    whole_basis = lax.all_gather(old_basis[0], "tensor", axis=0, tiled=True)
    turned = jnp.dot(summed, whole_basis, precision=highest)
    first_new = momentum_decay * first_moment[0] + (1.0 - momentum_decay) * turned
    second_new = square_decay * second_moment[0] + (1.0 - square_decay) * turned * turned
    direction = first_new / jnp.sqrt(second_new)
    rotated_back = lax.dot_general(
        direction, whole_basis, (((1,), (1,)), ((), ())), precision=highest
    )
    weight_new = master_weights[0] - step_size * rotated_back
    gathered = lax.all_gather(weight_new[None], "shard", axis=0, tiled=True)
    updated_weights = jnp.take(gathered, owner_table, axis=0)
    rows_here = old_basis.shape[1]
    position = lax.axis_index("tensor") * rows_here
    whole_grad = lax.all_gather(summed, "tensor", axis=0, tiled=True)
    own_columns = lax.dynamic_slice_in_dim(whole_grad, position, rows_here, 1)
    fresh_term = lax.dot_general(
        own_columns, whole_grad, (((0,), (0,)), ((), ())), precision=highest
    )
    stats_new = stats_decay * old_stats[0] + (1.0 - stats_decay) * fresh_term
    power_part = jnp.dot(stats_new, whole_basis, precision=highest)
    whole_power = lax.all_gather(power_part, "tensor", axis=0, tiled=True)
    gram_matrix = gram_of(whole_power)
    factor = start_gain / jnp.sqrt(jnp.trace(gram_matrix) + epsilon)
    current = whole_power * factor
    gram_matrix = gram_matrix * (factor * factor)
    for sweep in range(NS_ITERS):
        if sweep > 0:
            gram_matrix = gram_of(current)
        if sweep + 1 < NS_ITERS:
            current = 1.5 * current - 0.5 * jnp.dot(current, gram_matrix, precision=highest)
        else:
            own_rows = lax.dynamic_slice_in_dim(current, position, rows_here, 0)
            current = 1.5 * own_rows - 0.5 * jnp.dot(own_rows, gram_matrix, precision=highest)
    return (updated_weights, first_new[None], second_new[None], current[None], stats_new[None])


def solution(mesh):
    return jax.shard_map(
        body,
        mesh=mesh,
        in_specs=(
            P("shard", None, "tensor", None),
            P("shard", "tensor", None),
            P("shard", "tensor", None),
            P("shard", "tensor", None),
            P("shard", "tensor", None),
            P("shard", "tensor", None),
            P(),
        ),
        out_specs=(
            P(None, "tensor", None),
            P("shard", "tensor", None),
            P("shard", "tensor", None),
            P("shard", "tensor", None),
            P("shard", "tensor", None),
        ),
        check_vma=False,
    )
```

profile of v0, /device:TPU:2, one launch (start us, length us, event | category | flops | bytes accessed | tf_op | source)
XLA Modules:
  0.0 952.9 jit_solution(6312819126764942959)
XLA Ops:
  8.0 0.0 copy-start
  8.0 0.0 reduce-scatter.2.cloned.1.call-start
  8.1 0.8 select_reduce_fusion.1
  8.9 0.3 copy-done
  9.2 0.6 gather_fusion
  9.9 0.0 copy-start.4
  9.9 1.5 select_convert_fusion
  11.5 0.0 reduce-scatter.2.cloned.1.call-update
  11.5 0.0 copy-start.5
  11.5 0.0 copy-start.6
  11.5 0.0 copy-start.8
  11.5 0.0 all-gather.9.cloned.1.call-start
  11.6 0.5 all-gather.9.cloned.1.call-update
  12.1 0.0 all-gather.7.cloned.1.call-start
  12.1 765.6 %reduce-scatter.2.cloned.1.call-done = f32[1,8,512]{2,1,0:T(8,128)} async-done(((f32[128,8,512]{2,1,0:T(8,128)}), f32[1,8,512]{2,1,0:T(8,128)}) %reduce-scatter.2.cloned.1.call-update) | async-done | bytes 16400 | tf_op jit(solution)/shard_map/reduce_scatter | solution.py:29
  777.7 0.0 copy-start.7
  777.7 5.6 all-gather.2
  783.3 0.0 copy-done.4
  783.3 0.4 fusion.2
  783.7 0.0 copy-start.3
  783.7 0.0 copy-start.9
  783.7 0.0 all-gather.9.cloned.1.call-done
  783.8 0.0 copy-start.1
  783.8 2.7 fusion.6
  786.5 0.0 all-gather.7.cloned.1.call-update
  786.5 0.0 all-gather.11.cloned.1.call-start
  786.6 0.0 copy-done.7
  786.6 0.0 copy-done.1
  786.6 0.6 fusion.9
  787.2 0.0 copy-done.5
  787.2 0.0 copy-done.6
  787.2 0.0 copy-done.8
  787.2 1.6 fusion.5
  788.8 0.0 all-gather.11.cloned.1.call-update
  788.8 0.0 copy-done.9
  788.9 0.6 fusion.24
  789.5 21.0 %all-gather.7.cloned.1.call-done = f32[512,512]{1,0:T(8,128)} async-done(((f32[128,512]{1,0:T(8,128)}), f32[512,512]{1,0:T(8,128)}) %all-gather.7.cloned.1.call-update) | async-done | bytes 1048592 | tf_op jit(solution)/shard_map/all_gather | solution.py:52
  810.5 0.0 copy-start.2
  810.5 4.1 select_reduce_fusion
  814.6 0.0 copy-done.3
  815.3 0.0 copy-done.2
  815.3 1.9 fusion.1
  817.2 1.9 fusion.33
  819.1 1.9 fusion
  820.9 1.9 fusion.34
  822.8 1.4 fusion.4
  824.2 117.3 %all-gather.11.cloned.1.call-done = f32[1024,512]{1,0:T(8,128)} async-done(((f32[8,512]{1,0:T(8,128)}), f32[1024,512]{1,0:T(8,128)}) %all-gather.11.cloned.1.call-update) | async-done | bytes 2097168 | tf_op jit(solution)/shard_map/all_gather | solution.py:41
  941.5 2.3 gather_fusion.1
  943.8 1.5 broadcast_select_fusion
  (6 shorter events, 0.0 us)
Async XLA Ops:
  8.0 1.2 copy-start
  8.0 769.7 %reduce-scatter.2.cloned.1.call-start = ((), (), s32[]{:S(2)}) async-start(), calls=%async_computation.1 | async-start | bytes 2113536 | tf_op jit(solution)/shard_map/reduce_scatter | solution.py:29
  9.9 773.4 %copy-start.4 = (f32[1,128,512]{2,1,0:T(8,128)S(1)}, f32[1,128,512]{2,1,0:T(8,128)}, u32[]{:S(2)}) copy-start(f32[1,128,512]{2,1,0:T(8,128)} %param.12) | copy-start | bytes 786436
  11.5 775.7 %copy-start.5 = (f32[1,8,512]{2,1,0:T(8,128)S(1)}, f32[1,8,512]{2,1,0:T(8,128)}, u32[]{:S(2)}) copy-start(f32[1,8,512]{2,1,0:T(8,128)} %param.9) | copy-start | bytes 49156
  11.5 775.7 %copy-start.6 = (f32[1,8,512]{2,1,0:T(8,128)S(1)}, f32[1,8,512]{2,1,0:T(8,128)}, u32[]{:S(2)}) copy-start(f32[1,8,512]{2,1,0:T(8,128)} %param.10) | copy-start | bytes 49156
  11.5 775.7 %copy-start.8 = (f32[1,8,512]{2,1,0:T(8,128)S(1)}, f32[1,8,512]{2,1,0:T(8,128)}, u32[]{:S(2)}) copy-start(f32[1,8,512]{2,1,0:T(8,128)} %param.8) | copy-start | bytes 49156
  11.5 772.2 %all-gather.9.cloned.1.call-start = ((), (), s32[]{:S(2)}) async-start(), calls=%async_computation.3 | async-start | bytes 1310720 | tf_op jit(solution)/shard_map/all_gather | solution.py:32
  12.1 798.4 %all-gather.7.cloned.1.call-start = ((), (), s32[]{:S(2)}) async-start(), calls=%async_computation.2 | async-start | bytes 1310720 | tf_op jit(solution)/shard_map/all_gather | solution.py:52
  777.7 8.9 copy-start.7
  783.7 30.9 %copy-start.3 = (f32[128,512]{1,0:T(8,128)}, f32[128,512]{1,0:T(8,128)S(1)}, u32[]{:S(2)}) copy-start(f32[128,512]{1,0:T(8,128)S(1)} %fusion.2) | copy-start | bytes 786436
  783.7 5.1 copy-start.9
  783.8 2.8 copy-start.1
  786.5 155.0 %all-gather.11.cloned.1.call-start = ((), (), s32[]{:S(2)}) async-start(), calls=%async_computation.4 | async-start | bytes 2113536 | tf_op jit(solution)/shard_map/all_gather | solution.py:41
  810.5 4.8 copy-start.2
Sparse Core Ops, SparseCore 0:
  12.2 765.4 reduce-scatter.1
Sparse Core Ops, SparseCore 1:
  14.1 30.2 all-gather.8
  786.6 23.8 all-gather.6
  815.4 126.0 all-gather.10
where the time goes:
time: 953 us
  waiting for transfers between devices  904 us (95%)
  matrix products  18.4 us (2%)
  between operations  16.6 us (2%)
    reduce_scatter x1, waiting for transfers between devices, body(): lax.psum_scatter(ordered.astype(jnp.float32), 'shard', scatter_dimension=...  766 us
    all_gather x1, waiting for transfers between devices, body(): gathered = lax.all_gather(weight_new[None], 'shard', axis=0, tiled=True)  117 us
    all_gather x1, waiting for transfers between devices, body(): whole_power = lax.all_gather(power_part, 'tensor', axis=0, tiled=True)  21 us
  transfers between devices with their start and end apart: 4, of which 3 were waited for; matrix products, arithmetic and copies ran while one was open for 2% of the time, Pallas kernels for 0%

commit v1 on v0

--- a/solution.py
+++ b/solution.py
@@ -1,3 +1,4 @@
+import functools
 import jax
 import jax.numpy as jnp
 from jax import lax
@@ -10,6 +11,19 @@
 step_size = 0.05
 start_gain = 1.7
 epsilon = 1e-06
+
+
+def _link_forms(field_in, a_name):
+    prior = jnp.concatenate(
+        lax.all_to_all(
+            jnp.stack([field_in for _ in range(lax.axis_size(a_name))], axis=0), a_name, 0, 0
+        ),
+        axis=0,
+    )
+    return prior
+
+
+obtain_lots_all = functools.partial(_link_forms, a_name="tensor")
 
 
 def gram_of(matrix):
@@ -49,7 +63,7 @@
     )
     stats_new = stats_decay * old_stats[0] + (1.0 - stats_decay) * fresh_term
     power_part = jnp.dot(stats_new, whole_basis, precision=highest)
-    whole_power = lax.all_gather(power_part, "tensor", axis=0, tiled=True)
+    whole_power = obtain_lots_all(power_part)
     gram_matrix = gram_of(whole_power)
     factor = start_gain / jnp.sqrt(jnp.trace(gram_matrix) + epsilon)
     current = whole_power * factor

time: 953 us -> 918 us (0.963)
  waiting for transfers between devices: 904 us -> 866 us
    all_gather x1, waiting for transfers between devices: 117 us -> 85.8 us  [body(): gathered = lax.all_gather(weight_new[None], 'shard', axis=0, tiled=True)]
    all_gather x1, waiting for transfers between devices: 0.03 us -> 29.4 us  [body(): whole_basis = lax.all_gather(old_basis[0], 'tensor', axis=0, tiled=True)]
    reduce_scatter x1, waiting for transfers between devices: 766 us -> 737 us  [body(): lax.psum_scatter(ordered.astype(jnp.float32), 'shard', scatter_dimension=...]
    all_gather x1 -> x0, waiting for transfers between devices: 21 us -> none  [body(): whole_power = lax.all_gather(power_part, 'tensor', axis=0, tiled=True)]
    all_to_all x0 -> x1, waiting for transfers between devices: none -> 13.8 us  [_link_forms(): lax.all_to_all(jnp.stack([field_in for _ in range(lax.axis_size(a_name))]...]
  transfers between devices with their start and end apart: 4 -> 4, of which waited for: 3 -> 4; matrix products, arithmetic and copies ran while one was open for 2% -> 2% of each run, Pallas kernels for 0% -> 0%
where the time goes in v1:
time: 918 us
  waiting for transfers between devices  866 us (94%)
  matrix products  17.1 us (2%)
  between operations  16.4 us (2%)
    reduce_scatter x1, waiting for transfers between devices, body(): lax.psum_scatter(ordered.astype(jnp.float32), 'shard', scatter_dimension=...  737 us
    all_gather x1, waiting for transfers between devices, body(): gathered = lax.all_gather(weight_new[None], 'shard', axis=0, tiled=True)  85.8 us
    all_gather x1, waiting for transfers between devices, body(): whole_basis = lax.all_gather(old_basis[0], 'tensor', axis=0, tiled=True)  29.4 us
  transfers between devices with their start and end apart: 4, of which 4 were waited for; matrix products, arithmetic and copies ran while one was open for 2% of the time, Pallas kernels for 0%

profile of v1, /device:TPU:2, one launch (start us, length us, event | category | flops | bytes accessed | tf_op | source)
XLA Modules:
  0.0 917.7 jit_solution(13574296122828042371)
XLA Ops:
  8.0 0.0 copy-start
  8.0 0.0 all-gather.6.cloned.1.call-start
  8.1 0.7 all-gather.6.cloned.1.call-update
  8.7 0.0 reduce-scatter.2.cloned.1.call-start
  8.8 0.8 select_reduce_fusion.1
  9.6 0.0 copy-done
  9.6 0.6 gather_fusion
  10.3 1.5 select_convert_fusion
  11.8 0.0 copy-start.4
  11.8 0.0 copy-start.5
  11.8 0.0 copy-start.7
  11.8 0.0 copy-start.3
  11.8 0.0 reduce-scatter.2.cloned.1.call-update
  11.8 0.0 all-gather.8.cloned.1.call-start
  11.9 29.4 %all-gather.6.cloned.1.call-done = f32[1,512,512]{2,1,0:T(8,128)} async-done(((f32[1,128,512]{2,1,0:T(8,128)}), f32[1,512,512]{2,1,0:T(8,128)}) %all-gather.6.cloned.1.call-update) | async-done | bytes 1048592 | tf_op jit(solution)/shard_map/all_gather | solution.py:46
  41.3 0.0 copy-start.1
  41.3 736.8 %reduce-scatter.2.cloned.1.call-done = f32[1,8,512]{2,1,0:T(8,128)} async-done(((f32[128,8,512]{2,1,0:T(8,128)}), f32[1,8,512]{2,1,0:T(8,128)}) %reduce-scatter.2.cloned.1.call-update) | async-done | bytes 16400 | tf_op jit(solution)/shard_map/reduce_scatter | solution.py:43
  778.0 0.0 copy-start.6
  778.1 1.9 fusion.9
  779.9 0.0 copy-done.4
  779.9 0.0 copy-done.5
  779.9 0.0 copy-done.7
  779.9 2.8 fusion.5
  782.7 0.0 all-gather.8.cloned.1.call-update
  782.8 0.0 copy-done.6
  782.8 5.2 all-gather.2
  788.0 0.0 copy-done.3
  788.0 0.4 fusion.2
  788.5 0.0 copy-done.1
  788.5 0.0 copy-start.2
  788.5 0.7 fusion.6
  789.2 0.0 copy-start.8
  789.2 1.1 stack.2
  790.3 0.0 copy-done.2
  790.3 3.7 all-to-all-start
  794.0 0.0 copy-done.8
  794.1 0.6 fusion.22
  794.7 13.8 %all-to-all-done = f32[4,128,512]{2,1,0:T(8,128)S(1)} async-done(((f32[4,128,512]{2,1,0:T(8,128)}), f32[4,128,512]{2,1,0:T(8,128)S(1)}, u32[]{:S(2)}, u32[]{:S(2)}) %all-to-all-start) | async-done | bytes 1048608 | tf_op jit(solution)/shard_map/all_to_all | solution.py:18
  808.5 2.4 select_reduce_fusion
  811.6 0.1 broadcast_multiply_fusion
  811.7 1.9 fusion.1
  813.6 1.9 fusion.31
  815.5 1.9 fusion
  817.3 1.9 fusion.32
  819.2 1.4 fusion.4
  820.6 85.8 %all-gather.8.cloned.1.call-done = f32[1024,512]{1,0:T(8,128)} async-done(((f32[8,512]{1,0:T(8,128)}), f32[1024,512]{1,0:T(8,128)}) %all-gather.8.cloned.1.call-update) | async-done | bytes 2097168 | tf_op jit(solution)/shard_map/all_gather | solution.py:55
  906.4 2.3 gather_fusion.1
  908.7 1.5 broadcast_select_fusion
  (6 shorter events, 0.0 us)
Async XLA Ops:
  8.0 1.6 copy-start
  8.0 33.3 %all-gather.6.cloned.1.call-start = ((), (), s32[]{:S(2)}) async-start(), calls=%async_computation.3 | async-start | bytes 1310720 | tf_op jit(solution)/shard_map/all_gather | solution.py:46
  8.7 769.3 %reduce-scatter.2.cloned.1.call-start = ((), (), s32[]{:S(2)}) async-start(), calls=%async_computation.2 | async-start | bytes 2113536 | tf_op jit(solution)/shard_map/reduce_scatter | solution.py:43
  11.8 768.1 %copy-start.4 = (f32[1,8,512]{2,1,0:T(8,128)S(1)}, f32[1,8,512]{2,1,0:T(8,128)}, u32[]{:S(2)}) copy-start(f32[1,8,512]{2,1,0:T(8,128)} %param.9) | copy-start | bytes 49156
  11.8 768.1 %copy-start.5 = (f32[1,8,512]{2,1,0:T(8,128)S(1)}, f32[1,8,512]{2,1,0:T(8,128)}, u32[]{:S(2)}) copy-start(f32[1,8,512]{2,1,0:T(8,128)} %param.10) | copy-start | bytes 49156
  11.8 768.1 %copy-start.7 = (f32[1,8,512]{2,1,0:T(8,128)S(1)}, f32[1,8,512]{2,1,0:T(8,128)}, u32[]{:S(2)}) copy-start(f32[1,8,512]{2,1,0:T(8,128)} %param.8) | copy-start | bytes 49156
  11.8 776.2 %copy-start.3 = (f32[1,128,512]{2,1,0:T(8,128)S(1)}, f32[1,128,512]{2,1,0:T(8,128)}, u32[]{:S(2)}) copy-start(f32[1,128,512]{2,1,0:T(8,128)} %param.12) | copy-start | bytes 786436
  11.8 894.6 %all-gather.8.cloned.1.call-start = ((), (), s32[]{:S(2)}) async-start(), calls=%async_computation.4 | async-start | bytes 2113536 | tf_op jit(solution)/shard_map/all_gather | solution.py:55
  41.3 747.2 %copy-start.1 = (f32[1,512,512]{2,1,0:T(8,128)S(1)}, f32[1,512,512]{2,1,0:T(8,128)}, u32[]{:S(2)}) copy-start(f32[1,512,512]{2,1,0:T(8,128)} %all-gather.6.cloned.1.call-done) | copy-start | bytes 3145732
  778.0 4.7 copy-start.6
  788.5 1.8 copy-start.2
  789.2 4.8 copy-start.8
  790.3 18.1 %all-to-all-start = ((f32[4,128,512]{2,1,0:T(8,128)}), f32[4,128,512]{2,1,0:T(8,128)S(1)}, u32[]{:S(2)}, u32[]{:S(2)}) async-start(f32[4,128,512]{2,1,0:T(8,128)} %stack.2), calls=%async_computation.1 | async-start | bytes 2097152 | tf_op jit(solution)/shard_map/all_to_all | solution.py:18
Sparse Core Ops, SparseCore 0:
  10.9 30.3 all-gather.5
Sparse Core Ops, SparseCore 1:
  12.6 765.4 reduce-scatter.1
  782.8 123.5 all-gather.7
